TPU v7x, 32 devices: a whole 2x2x4 slice. The times are simulated.
32 devices in a mesh: fsdp: 8 (over y, x, core), seq: 4 (over z).
Axes of the slice: x: 2, y: 2, z: 4, core: 2. Of those that a mesh axis runs over, the one named last changes fastest.
Arguments:
- inputs: bfloat16 [8, 1568, 1024], P('fsdp', 'seq'), may hold values from -6 to 6
- clip_mask: int32 [8], P('fsdp'), may hold values 0 or 1
- ln1_gain: float32 [1024], replicated, may hold values from 0.5 to 1.5
- ln1_bias: float32 [1024], replicated, may hold values from -1 to 1
- w_query: bfloat16 [1024, 1024], P('fsdp'), may hold values from -0.1875 to 0.1875
- b_query: float32 [1024], replicated, may hold values from -1 to 1
- w_key: bfloat16 [1024, 1024], P('fsdp'), may hold values from -0.1875 to 0.1875
- w_value: bfloat16 [1024, 1024], P('fsdp'), may hold values from -0.1875 to 0.1875
- b_value: float32 [1024], replicated, may hold values from -1 to 1
- w_out: bfloat16 [1024, 1024], P('fsdp'), may hold values from -3 to 3
- b_out: float32 [1024], replicated, may hold values from -1 to 1
- ln2_gain: float32 [1024], replicated, may hold values from 0.5 to 1.5
- ln2_bias: float32 [1024], replicated, may hold values from -1 to 1
- w_fc1: bfloat16 [1024, 4096], P('fsdp'), may hold values from -0.1875 to 0.1875
- b_fc1: float32 [4096], replicated, may hold values from -1 to 1
- w_fc2: bfloat16 [4096, 1024], P('fsdp'), may hold values from -0.09375 to 0.09375
- b_fc2: float32 [1024], replicated, may hold values from -1 to 1
- cotangent: bfloat16 [8, 1568, 1024], P('fsdp', 'seq'), may hold values from -6 to 6
Outputs:
- output: bfloat16 [8, 1568, 1024], P('fsdp', 'seq')
- grad_inputs: float32 [8, 1568, 1024], P('fsdp', 'seq')
- grad_ln1_gain: float32 [1024], P(('fsdp', 'seq'))
- grad_ln1_bias: float32 [1024], P(('fsdp', 'seq'))
- grad_w_query: float32 [1024, 1024], P(('fsdp', 'seq'))
- grad_b_query: float32 [1024], P(('fsdp', 'seq'))
- grad_w_key: float32 [1024, 1024], P(('fsdp', 'seq'))
- grad_w_value: float32 [1024, 1024], P(('fsdp', 'seq'))
- grad_b_value: float32 [1024], P(('fsdp', 'seq'))
- grad_w_out: float32 [1024, 1024], P(('fsdp', 'seq'))
- grad_b_out: float32 [1024], P(('fsdp', 'seq'))
- grad_ln2_gain: float32 [1024], P(('fsdp', 'seq'))
- grad_ln2_bias: float32 [1024], P(('fsdp', 'seq'))
- grad_w_fc1: float32 [1024, 4096], P(('fsdp', 'seq'))
- grad_b_fc1: float32 [4096], P(('fsdp', 'seq'))
- grad_w_fc2: float32 [4096, 1024], P(('fsdp', 'seq'))
- grad_b_fc2: float32 [1024], P(('fsdp', 'seq'))
Inputs may be any that keep to these rules, and one draw needn't show every extreme that they name: `clip_mask`: 1 where the clip's slot holds a clip, 0 where it holds none.
All inputs are finite; a program needn't handle non-finite values. No bound on the sum of `clip_mask` on one device may be relied on, other than what follows from the above.
Results may differ from a plain program's by a relative error of at most 0.011.
Values may be sent and summed in bfloat16 or wider, within the bound.
No kernel may reach another device: no remote copies, remote signals or barrier semaphores. Data moves between devices by JAX's collectives and lax.ppermute only.
A program may use at most 256 MiB of HBM per device.

v0:
```python
import jax
import jax.numpy as jnp
from jax import lax
from jax.sharding import PartitionSpec as P

HEADS = 16
HD = 64
EPSILON = 1e-06


def normalize(rows, gain, shift):
    center = rows - jnp.mean(rows, -1, keepdims=True)
    inverse = lax.rsqrt(jnp.mean(center * center, -1, keepdims=True) + EPSILON)
    normed = center * inverse
    return (normed * gain + shift, normed, inverse)


def norm_grad(grad, normed, inverse, gain):
    scaled = grad * gain
    inner = (
        scaled
        - jnp.mean(scaled, -1, keepdims=True)
        - normed * jnp.mean(scaled * normed, -1, keepdims=True)
    )
    return inner * inverse


def to_pairs(array):
    clips, length, heads_here, size = array.shape
    return array.transpose(0, 2, 1, 3).reshape(clips * heads_here, length, size)


def from_pairs(array, clips):
    pairs, length, size = array.shape
    return array.reshape(clips, pairs // clips, length, size).transpose(0, 2, 1, 3)


def head_forward(blocks):
    query, keys, values = blocks
    scale = query.shape[-1] ** (-0.5)
    scores = jnp.dot(query, keys.T, preferred_element_type=jnp.float32) * scale
    peak = jnp.max(scores, -1, keepdims=True)
    expo = jnp.exp(scores - peak)
    total = jnp.sum(expo, -1, keepdims=True)
    weights = (expo / total).astype(jnp.bfloat16)
    mixed = jnp.dot(weights, values, preferred_element_type=jnp.float32).astype(jnp.bfloat16)
    return (mixed, (peak + jnp.log(total))[:, 0])


def head_backward(blocks):
    query, keys, values, grad_out, logsum = blocks
    scale = query.shape[-1] ** (-0.5)
    scores = jnp.dot(query, keys.T, preferred_element_type=jnp.float32) * scale
    probs = jnp.exp(scores - logsum[:, None])
    grad_probs = jnp.dot(grad_out, values.T, preferred_element_type=jnp.float32)
    inner = jnp.sum(probs * grad_probs, -1, keepdims=True)
    grad_scores = (probs * (grad_probs - inner)).astype(jnp.bfloat16)
    grad_query = (jnp.dot(grad_scores, keys, preferred_element_type=jnp.float32) * scale).astype(
        jnp.bfloat16
    )
    grad_keys = (jnp.dot(grad_scores.T, query, preferred_element_type=jnp.float32) * scale).astype(
        jnp.bfloat16
    )
    grad_values = jnp.dot(
        probs.astype(jnp.bfloat16).T, grad_out, preferred_element_type=jnp.float32
    ).astype(jnp.bfloat16)
    return (grad_query, grad_keys, grad_values)


def run_forward(inputs, mask_rows, vectors, attn_mats, mlp_mats):
    ln1_gain, ln1_bias, b_query, b_value, b_out, ln2_gain, ln2_bias, b_fc1, b_fc2 = vectors
    w_query, w_key, w_value, w_out = attn_mats
    w_fc1, w_fc2 = mlp_mats
    clips, local_len, width = inputs.shape
    rows = inputs.reshape(clips * local_len, width).astype(jnp.float32)
    normed1, hat1, inv1 = normalize(rows, ln1_gain, ln1_bias)
    first_in = normed1.astype(jnp.bfloat16)
    head_shape = (clips, local_len, HEADS, HD)
    query = (jnp.dot(first_in, w_query, preferred_element_type=jnp.float32) + b_query).astype(
        jnp.bfloat16
    )
    keys = jnp.dot(first_in, w_key, preferred_element_type=jnp.float32).astype(jnp.bfloat16)
    values = (jnp.dot(first_in, w_value, preferred_element_type=jnp.float32) + b_value).astype(
        jnp.bfloat16
    )
    query_heads, keys_heads, values_heads = (
        lax.all_to_all(query.reshape(head_shape), "seq", split_axis=2, concat_axis=1, tiled=True),
        lax.all_to_all(keys.reshape(head_shape), "seq", split_axis=2, concat_axis=1, tiled=True),
        lax.all_to_all(values.reshape(head_shape), "seq", split_axis=2, concat_axis=1, tiled=True),
    )
    query_pairs = to_pairs(query_heads)
    keys_pairs = to_pairs(keys_heads)
    values_pairs = to_pairs(values_heads)
    mixed_pairs, logsum = lax.map(head_forward, (query_pairs, keys_pairs, values_pairs))
    mixed_tokens = lax.all_to_all(
        from_pairs(mixed_pairs, clips), "seq", split_axis=1, concat_axis=2, tiled=True
    )
    attended = mixed_tokens.reshape(clips * local_len, width)
    branch = jnp.dot(attended, w_out, preferred_element_type=jnp.float32) + b_out
    middle = rows + branch
    normed2, hat2, inv2 = normalize(middle, ln2_gain, ln2_bias)
    second_in = normed2.astype(jnp.bfloat16)
    hidden = jnp.dot(second_in, w_fc1, preferred_element_type=jnp.float32) + b_fc1
    activ = jax.nn.gelu(hidden, approximate=False).astype(jnp.bfloat16)
    final = jnp.dot(activ, w_fc2, preferred_element_type=jnp.float32) + b_fc2
    result = (middle + final) * mask_rows
    saved = (
        first_in,
        hat1,
        inv1,
        query_pairs,
        keys_pairs,
        values_pairs,
        logsum,
        attended,
        second_in,
        hat2,
        inv2,
        hidden,
        activ,
    )
    return (result, saved)


def on_device(
    inputs,
    clip_mask,
    ln1_gain,
    ln1_bias,
    w_query,
    b_query,
    w_key,
    w_value,
    b_value,
    w_out,
    b_out,
    ln2_gain,
    ln2_bias,
    w_fc1,
    b_fc1,
    w_fc2,
    b_fc2,
    cotangent,
):
    clips, local_len, width = inputs.shape
    mask_rows = jnp.repeat(clip_mask.astype(jnp.float32), local_len)[:, None]
    vectors = (ln1_gain, ln1_bias, b_query, b_value, b_out, ln2_gain, ln2_bias, b_fc1, b_fc2)
    attn_mats = (
        lax.all_gather(w_query, "fsdp", axis=0, tiled=True),
        lax.all_gather(w_key, "fsdp", axis=0, tiled=True),
        lax.all_gather(w_value, "fsdp", axis=0, tiled=True),
        lax.all_gather(w_out, "fsdp", axis=0, tiled=True),
    )
    mlp_mats = (
        lax.all_gather(w_fc1, "fsdp", axis=0, tiled=True),
        lax.all_gather(w_fc2, "fsdp", axis=0, tiled=True),
    )
    result, unused = run_forward(inputs, mask_rows, vectors, attn_mats, mlp_mats)
    output = result.reshape(clips, local_len, width).astype(jnp.bfloat16)
    attn_back = (
        lax.all_gather(w_query, "fsdp", axis=0, tiled=True),
        lax.all_gather(w_key, "fsdp", axis=0, tiled=True),
        lax.all_gather(w_value, "fsdp", axis=0, tiled=True),
        lax.all_gather(w_out, "fsdp", axis=0, tiled=True),
    )
    mlp_back = (
        lax.all_gather(w_fc1, "fsdp", axis=0, tiled=True),
        lax.all_gather(w_fc2, "fsdp", axis=0, tiled=True),
    )
    full_query, full_key, full_value, full_out = attn_back
    full_fc1, full_fc2 = mlp_back
    unused_result, saved = run_forward(inputs, mask_rows, vectors, attn_back, mlp_back)
    (
        first_in,
        hat1,
        inv1,
        query_pairs,
        keys_pairs,
        values_pairs,
        logsum,
        attended,
        second_in,
        hat2,
        inv2,
        hidden,
        activ,
    ) = saved
    grad_rows = cotangent.reshape(clips * local_len, width).astype(jnp.float32) * mask_rows
    grad_low = grad_rows.astype(jnp.bfloat16)
    grad_b_fc2 = jnp.sum(grad_rows, 0)
    grad_w_fc2 = jnp.dot(activ.T, grad_low, preferred_element_type=jnp.float32)
    grad_activ = jnp.dot(grad_low, full_fc2.T, preferred_element_type=jnp.float32)
    unused_gelu, gelu_pull = jax.vjp(lambda value: jax.nn.gelu(value, approximate=False), hidden)
    grad_hidden = gelu_pull(grad_activ)[0].astype(jnp.bfloat16)
    grad_w_fc1 = jnp.dot(second_in.T, grad_hidden, preferred_element_type=jnp.float32)
    grad_b_fc1 = jnp.sum(grad_hidden.astype(jnp.float32), 0)
    grad_second = jnp.dot(grad_hidden, full_fc1.T, preferred_element_type=jnp.float32)
    grad_ln2_gain = jnp.sum(grad_second * hat2, 0)
    grad_ln2_bias = jnp.sum(grad_second, 0)
    grad_middle = grad_rows + norm_grad(grad_second, hat2, inv2, ln2_gain)
    grad_branch = grad_middle.astype(jnp.bfloat16)
    grad_w_out = jnp.dot(attended.T, grad_branch, preferred_element_type=jnp.float32)
    grad_b_out = jnp.sum(grad_branch.astype(jnp.float32), 0)
    grad_mixed = jnp.dot(grad_branch, full_out.T, preferred_element_type=jnp.float32).astype(
        jnp.bfloat16
    )
    grad_mixed_heads = lax.all_to_all(
        grad_mixed.reshape(clips, local_len, HEADS, HD),
        "seq",
        split_axis=2,
        concat_axis=1,
        tiled=True,
    )
    grad_q_pairs, grad_k_pairs, grad_v_pairs = lax.map(
        head_backward, (query_pairs, keys_pairs, values_pairs, to_pairs(grad_mixed_heads), logsum)
    )
    grad_query, grad_keys, grad_values = (
        lax.all_to_all(
            from_pairs(grad_q_pairs, clips), "seq", split_axis=1, concat_axis=2, tiled=True
        ),
        lax.all_to_all(
            from_pairs(grad_k_pairs, clips), "seq", split_axis=1, concat_axis=2, tiled=True
        ),
        lax.all_to_all(
            from_pairs(grad_v_pairs, clips), "seq", split_axis=1, concat_axis=2, tiled=True
        ),
    )
    grad_query = grad_query.reshape(clips * local_len, width)
    grad_keys = grad_keys.reshape(clips * local_len, width)
    grad_values = grad_values.reshape(clips * local_len, width)
    grad_w_query = jnp.dot(first_in.T, grad_query, preferred_element_type=jnp.float32)
    grad_w_key = jnp.dot(first_in.T, grad_keys, preferred_element_type=jnp.float32)
    grad_w_value = jnp.dot(first_in.T, grad_values, preferred_element_type=jnp.float32)
    grad_b_query = jnp.sum(grad_query.astype(jnp.float32), 0)
    grad_b_value = jnp.sum(grad_values.astype(jnp.float32), 0)
    grad_first = (
        jnp.dot(grad_query, full_query.T, preferred_element_type=jnp.float32)
        + jnp.dot(grad_keys, full_key.T, preferred_element_type=jnp.float32)
        + jnp.dot(grad_values, full_value.T, preferred_element_type=jnp.float32)
    )
    grad_ln1_gain = jnp.sum(grad_first * hat1, 0)
    grad_ln1_bias = jnp.sum(grad_first, 0)
    grad_inputs = grad_middle + norm_grad(grad_first, hat1, inv1, ln1_gain)
    grad_inputs = grad_inputs.reshape(clips, local_len, width)
    all_grads = (
        grad_ln1_gain,
        grad_ln1_bias,
        grad_w_query,
        grad_b_query,
        grad_w_key,
        grad_w_value,
        grad_b_value,
        grad_w_out,
        grad_b_out,
        grad_ln2_gain,
        grad_ln2_bias,
        grad_w_fc1,
        grad_b_fc1,
        grad_w_fc2,
        grad_b_fc2,
    )
    owned = (
        lax.psum_scatter(all_grads[0], ("fsdp", "seq"), scatter_dimension=0, tiled=True),
        lax.psum_scatter(all_grads[1], ("fsdp", "seq"), scatter_dimension=0, tiled=True),
        lax.psum_scatter(all_grads[2], ("fsdp", "seq"), scatter_dimension=0, tiled=True),
        lax.psum_scatter(all_grads[3], ("fsdp", "seq"), scatter_dimension=0, tiled=True),
        lax.psum_scatter(all_grads[4], ("fsdp", "seq"), scatter_dimension=0, tiled=True),
        lax.psum_scatter(all_grads[5], ("fsdp", "seq"), scatter_dimension=0, tiled=True),
        lax.psum_scatter(all_grads[6], ("fsdp", "seq"), scatter_dimension=0, tiled=True),
        lax.psum_scatter(all_grads[7], ("fsdp", "seq"), scatter_dimension=0, tiled=True),
        lax.psum_scatter(all_grads[8], ("fsdp", "seq"), scatter_dimension=0, tiled=True),
        lax.psum_scatter(all_grads[9], ("fsdp", "seq"), scatter_dimension=0, tiled=True),
        lax.psum_scatter(all_grads[10], ("fsdp", "seq"), scatter_dimension=0, tiled=True),
        lax.psum_scatter(all_grads[11], ("fsdp", "seq"), scatter_dimension=0, tiled=True),
        lax.psum_scatter(all_grads[12], ("fsdp", "seq"), scatter_dimension=0, tiled=True),
        lax.psum_scatter(all_grads[13], ("fsdp", "seq"), scatter_dimension=0, tiled=True),
        lax.psum_scatter(all_grads[14], ("fsdp", "seq"), scatter_dimension=0, tiled=True),
    )
    return (
        output,
        grad_inputs,
        owned[0],
        owned[1],
        owned[2],
        owned[3],
        owned[4],
        owned[5],
        owned[6],
        owned[7],
        owned[8],
        owned[9],
        owned[10],
        owned[11],
        owned[12],
        owned[13],
        owned[14],
    )


def solution(mesh):
    return jax.shard_map(
        on_device,
        mesh=mesh,
        in_specs=(
            P("fsdp", "seq", None),
            P("fsdp"),
            P(),
            P(),
            P("fsdp", None),
            P(),
            P("fsdp", None),
            P("fsdp", None),
            P(),
            P("fsdp", None),
            P(),
            P(),
            P(),
            P("fsdp", None),
            P(),
            P("fsdp", None),
            P(),
            P("fsdp", "seq", None),
        ),
        out_specs=(
            P("fsdp", "seq", None),
            P("fsdp", "seq", None),
            P(("fsdp", "seq")),
            P(("fsdp", "seq")),
            P(("fsdp", "seq"), None),
            P(("fsdp", "seq")),
            P(("fsdp", "seq"), None),
            P(("fsdp", "seq"), None),
            P(("fsdp", "seq")),
            P(("fsdp", "seq"), None),
            P(("fsdp", "seq")),
            P(("fsdp", "seq")),
            P(("fsdp", "seq")),
            P(("fsdp", "seq"), None),
            P(("fsdp", "seq")),
            P(("fsdp", "seq"), None),
            P(("fsdp", "seq")),
        ),
        check_vma=False,
    )
```

profile of v0, /device:TPU:0, one launch (start us, length us, event | category | flops | bytes accessed | tf_op | source)
XLA Modules:
  0.0 1689.8 jit_solution(14784483086480142402)
XLA Ops:
  13.5 27.1 %all-gather.7.cloned.1.call-done = bf16[1024,1024]{1,0:T(8,128)(2,1)} async-done(((bf16[128,1024]{1,0:T(8,128)(2,1)}), bf16[1024,1024]{1,0:T(8,128)(2,1)}) %all-gather.7.cloned.1.call-update) | async-done | bytes 2097168 | tf_op jit(solution)/shard_map/all_gather | solution.py:149
  49.5 20.9 %all-gather.9.cloned.1.call-done = bf16[1024,1024]{1,0:T(8,128)(2,1)} async-done(((bf16[128,1024]{1,0:T(8,128)(2,1)}), bf16[1024,1024]{1,0:T(8,128)(2,1)}) %all-gather.9.cloned.1.call-update) | async-done | bytes 2097168 | tf_op jit(solution)/shard_map/all_gather | solution.py:150
  79.9 20.3 %all-gather.11.cloned.1.call-done = bf16[1024,1024]{1,0:T(8,128)(2,1)} async-done(((bf16[128,1024]{1,0:T(8,128)(2,1)}), bf16[1024,1024]{1,0:T(8,128)(2,1)}) %all-gather.11.cloned.1.call-update) | async-done | bytes 2097168 | tf_op jit(solution)/shard_map/all_gather | solution.py:151
  113.1 22.1 %all-to-all-done.2 = bf16[1,392,16,64]{1,3,0,2:T(8,128)(2,1)} async-done(((bf16[1,392,16,64]{1,3,0,2:T(8,128)(2,1)}), bf16[1,392,16,64]{1,3,0,2:T(8,128)(2,1)}, u32[]{:S(2)}, u32[]{:S(2)}) %all-to-all-start.2) | async-done | bytes 802848 | tf_op jit(solution)/shard_map/all_to_all | solution.py:89
  138.7 29.4 %while.37 = (s32[]{:T(128)}, bf16[4,1568,64]{1,2,0:T(8,128)(2,1)}, f32[4,1568]{1,0:T(4,128)S(1)}, bf16[4,1568,64]{2,1,0:T(8,128)(2,1)S(1)}, bf16[4,1568,64]{2,1,...) while((s32[]{:T(128)}, bf16[4,1568,64]{1,2,0:T(8,128)(2,1)}, ...), condition=%wide.region_11.12_spmd, body=%wide.region_8.0_spmd.sunk | while | flops 651634176 | bytes 30998112 | solution.py:94
  183.5 19.4 %all-to-all-done.4 = bf16[4,2,50176]{2,1,0:T(2,128)(2,1)} async-done(((bf16[4,2,50176]{2,1,0:T(2,128)(2,1)}), bf16[4,2,50176]{2,1,0:T(2,128)(2,1)}, u32[]{:S(2)}, u32[]{:S(2)}) %all-to-all-start.4) | async-done | bytes 802848 | tf_op jit(solution)/shard_map/all_to_all | solution.py:95
  215.6 21.5 %fusion.70 = (f32[392,4096]{1,0:T(8,128)}, f32[392,4096]{1,0:T(8,128)}) fusion(f32[4096]{0:T(1024)S(1)} %copy-done.16, bf16[1024,4096]{1,0:T(8,128)(2,1)} %all-gather.15.cloned.1.call-done, f32[392,1024]{1,0:T(8,128)} %copy-done.4, f32[392]{0:T(512)S(1)} %add_rsqrt_fusion, f32[392]{0:T(512)S(1)} %broadcast_multiply_fusion.4, f32[1024]{0:T(1024)S(1)} %copy-done.45, ...), kind=kOutput, calls=%fused_computation.79 | convolution fusion | flops 3391496192 | bytes 22867008 | tf_op jit(solution)/shard_map/dot_general | solution.py:103
  242.2 11.8 convert_reduce_fusion
  274.7 34.4 %all-to-all-done.5 = bf16[1,392,16,64]{1,3,0,2:T(8,128)(2,1)} async-done(((bf16[1,392,16,64]{1,3,0,2:T(8,128)(2,1)}), bf16[1,392,16,64]{1,3,0,2:T(8,128)(2,1)}, u32[]{:S(2)}, u32[]{:S(2)}) %all-to-all-start.5) | async-done | bytes 802848 | tf_op jit(solution)/shard_map/all_to_all | solution.py:207
  315.2 131.6 %while.38 = (s32[]{:T(128)}, bf16[4,1568,64]{1,2,0:T(8,128)(2,1)}, bf16[4,1568,64]{1,2,0:T(8,128)(2,1)}, bf16[4,1568,64]{1,2,0:T(8,128)(2,1)}, bf16[4,1568,64]{2...) while((s32[]{:T(128)}, bf16[4,1568,64]{1,2,0:T(8,128)(2,1)}, ...), condition=%wide.region_18.19_spmd, body=%wide.region_16.18_spmd.sunk | while | flops 1593688576 | bytes 157126304 | solution.py:214
  317.9 5.7 multiply_reduce_fusion.14
  324.8 10.5 multiply_convert_fusion.5
  350.8 5.8 multiply_reduce_fusion.14
  357.7 10.5 multiply_convert_fusion.5
  383.7 5.7 multiply_reduce_fusion.14
  390.6 10.5 multiply_convert_fusion.5
  416.6 5.8 multiply_reduce_fusion.14
  423.6 10.5 multiply_convert_fusion.5
  457.1 21.4 %all_to_all.162 = bf16[4,2,50176]{2,1,0:T(2,128)(2,1)} all-to-all(bf16[4,2,50176]{2,1,0:T(2,128)(2,1)} %reshape.302), channel_id=1, replica_groups=mesh['fsdp'=8,'seq'=4] {'seq'}, dimensions={0} | all-to-all | bytes 1605632 | tf_op jit(solution)/shard_map/all_to_all | solution.py:218
  501.9 40.5 %all_to_all.163 = bf16[4,2,50176]{2,1,0:T(2,128)(2,1)} all-to-all(bf16[4,2,50176]{2,1,0:T(2,128)(2,1)} %reshape.304), channel_id=1, replica_groups=mesh['fsdp'=8,'seq'=4] {'seq'}, dimensions={0} | all-to-all | bytes 1605632 | tf_op jit(solution)/shard_map/all_to_all | solution.py:221
  550.3 5.1 fusion.186
  565.8 39.4 %all_to_all.164 = bf16[4,2,50176]{2,1,0:T(2,128)(2,1)} all-to-all(bf16[4,2,50176]{2,1,0:T(2,128)(2,1)} %reshape.306), channel_id=1, replica_groups=mesh['fsdp'=8,'seq'=4] {'seq'}, dimensions={0} | all-to-all | bytes 1605632 | tf_op jit(solution)/shard_map/all_to_all | solution.py:224
  613.1 5.1 fusion.184
  619.0 13.0 fusion.182
  632.7 15.5 fusion.83
  649.1 28.9 %while.36 = (s32[]{:T(128)}, bf16[4,1568,64]{1,2,0:T(8,128)(2,1)}, bf16[4,1568,64]{2,1,0:T(8,128)(2,1)S(1)}, bf16[4,1568,64]{2,1,0:T(8,128)(2,1)S(1)}, bf16[4,1568,64]{2,1,0:T(8,128)(2,1)}, /*index=5*/s32[]{:T(128)}) while((s32[]{:T(128)}, bf16[4,1568,64]{1,2,0:T(8,128)(2,1)}, bf16[4,1568,64]{2,1,0:T(8,128)(2,1)S(1)}, ...), condition=%wide.region_5.6_spmd, body=%wide.region_2.5_spmd.sunk | while | flops 651632576 | bytes 30954188 | solution.py:94
  690.8 33.4 %all-to-all-done.3 = bf16[4,2,50176]{2,1,0:T(2,128)(2,1)S(1)} async-done(((bf16[4,2,50176]{2,1,0:T(2,128)(2,1)}), bf16[4,2,50176]{2,1,0:T(2,128)(2,1)S(1)}, u32[]{:S(2)}, u32[]{:S(2)}) %all-to-all-start.3) | async-done | bytes 802848 | tf_op jit(solution)/shard_map/all_to_all | solution.py:95
  730.1 26.3 %fusion.137 = bf16[1,392,1024]{2,1,0:T(8,128)(2,1)} fusion(f32[392,1024]{1,0:T(8,128)S(1)} %get-tuple-element.198, bf16[4096,1024]{1,0:T(8,128)(2,1)} %all-gather.17.cloned.1.call-done, bf16[1024,4096]{1,0:T(8,128)(2,1)} %all-gather.15.cloned.1.call-done, f32[4096]{0:T(1024)S(1)} %copy-done.17, f32[]{:T(128)} %bitcast.42, f32[1024]{0:T(1024)S(1)} %copy-done.44, ...), kind=kOutput, calls=%fused_computation.189 | convolution fusion | flops 6686253056 | bytes 19217476 | tf_op jit(solution)/shard_map/dot_general | solution.py:105
  766.5 39.0 %all-reduce.9 = (f32[1024]{0:T(1024)S(1)}, f32[1024]{0:T(1024)S(1)}, f32[1024]{0:T(1024)S(1)}, f32[1024]{0:T(1024)S(1)}, f32[1024]{0:T(1024)S(1)}, /*index=5*/f3...) all-reduce(f32[1024]{0:T(1024)S(1)} %get-tuple-element.134, ...), channel_id=2, replica_groups=mesh['fsdp'=8,'seq'=4] {'fsdp','seq'}, use_global_device_ids=true, to_apply=%region_22.23.clone | all-reduce | flops 12288 | bytes 98304
  813.9 138.1 %reduce-scatter.11.cloned.1.call-done = f32[32,1024]{1,0:T(8,128)} async-done(((f32[1024,1024]{1,0:T(8,128)}), f32[32,1024]{1,0:T(8,128)}) %reduce-scatter.11.cloned.1.call-update) | async-done | bytes 131088 | tf_op jit(solution)/shard_map/reduce_scatter | solution.py:268
  952.1 365.8 %reduce-scatter.15.cloned.1.call-done = f32[32,4096]{1,0:T(8,128)} async-done(((f32[1024,4096]{1,0:T(8,128)}), f32[32,4096]{1,0:T(8,128)}) %reduce-scatter.15.cloned.1.call-update) | async-done | bytes 524304 | tf_op jit(solution)/shard_map/reduce_scatter | solution.py:274
  1317.9 364.9 %reduce-scatter.17.cloned.1.call-done = f32[128,1024]{1,0:T(8,128)} async-done(((f32[4096,1024]{1,0:T(8,128)}), f32[128,1024]{1,0:T(8,128)}) %reduce-scatter.17.cloned.1.call-update) | async-done | bytes 524304 | tf_op jit(solution)/shard_map/reduce_scatter | solution.py:276
  (284 shorter events, 324.0 us)
Async XLA Ops:
  7.2 33.4 %all-gather.7.cloned.1.call-start = ((), (), s32[]{:S(2)}) async-start(), calls=%async_computation.15 | async-start | bytes 2359296 | tf_op jit(solution)/shard_map/all_gather | solution.py:149
  7.9 62.4 %all-gather.9.cloned.1.call-start = ((), (), s32[]{:S(2)}) async-start(), calls=%async_computation.16 | async-start | bytes 2359296 | tf_op jit(solution)/shard_map/all_gather | solution.py:150
  8.7 91.5 %all-gather.11.cloned.1.call-start = ((), (), s32[]{:S(2)}) async-start(), calls=%async_computation.17 | async-start | bytes 2359296 | tf_op jit(solution)/shard_map/all_gather | solution.py:151
  9.4 201.4 %all-gather.13.cloned.1.call-start = ((), (), s32[]{:S(2)}) async-start(), calls=%async_computation.18 | async-start | bytes 2359296 | tf_op jit(solution)/shard_map/all_gather | solution.py:152
  10.0 205.6 %all-gather.15.cloned.1.call-start = ((), (), s32[]{:S(2)}) async-start(), calls=%async_computation.19 | async-start | bytes 9437184 | tf_op jit(solution)/shard_map/all_gather | solution.py:155
  11.9 88.3 %copy-start.18 = (f32[392]{0:T(512)}, f32[392]{0:T(512)S(1)}, u32[]{:S(2)}) copy-start(f32[392]{0:T(512)S(1)} %broadcast_multiply_fusion.6) | copy-start | bytes 4708
  13.4 86.8 %copy-start.25 = (f32[392]{0:T(512)}, f32[392]{0:T(512)S(1)}, u32[]{:S(2)}) copy-start(f32[392]{0:T(512)S(1)} %add_rsqrt_fusion.2) | copy-start | bytes 4708
  13.4 56.9 %copy-start.2 = (bf16[1,392,1024]{2,1,0:T(8,128)(2,1)S(1)}, bf16[1,392,1024]{2,1,0:T(8,128)(2,1)}, u32[]{:S(2)}) copy-start(bf16[1,392,1024]{2,1,0:T(8,128)(2,1)} %param.24) | copy-start | bytes 2408452
  13.4 56.9 %copy-start.30 = (f32[1024]{0:T(1024)S(1)}, f32[1024]{0:T(1024)}, u32[]{:S(2)}) copy-start(f32[1024]{0:T(1024)} %param.26) | copy-start | bytes 12292
  13.4 56.9 %copy-start.42 = (f32[1024]{0:T(1024)S(1)}, f32[1024]{0:T(1024)}, u32[]{:S(2)}) copy-start(f32[1024]{0:T(1024)} %param.27) | copy-start | bytes 12292
  44.8 30.8 %all-to-all-start = ((bf16[1,392,16,64]{1,3,0,2:T(8,128)(2,1)}), bf16[1,392,16,64]{1,3,0,2:T(8,128)(2,1)S(1)}, u32[]{:S(2)}, u32[]{:S(2)}) async-start(bf16[1,392,16,64]{1,3,0,2:T(8,128)(2,1)} %bitcast.17), calls=%async_computation | async-start | bytes 2097152 | tf_op jit(solution)/shard_map/all_to_all | solution.py:87
  49.5 50.7 %copy-start.41 = (f32[1024]{0:T(1024)S(1)}, f32[1024]{0:T(1024)}, u32[]{:S(2)}) copy-start(f32[1024]{0:T(1024)} %param.32) | copy-start | bytes 12292
  75.6 29.7 %all-to-all-start.1 = ((bf16[1,392,16,64]{1,3,0,2:T(8,128)(2,1)}), bf16[1,392,16,64]{1,3,0,2:T(8,128)(2,1)}, u32[]{:S(2)}, u32[]{:S(2)}) async-start(bf16[1,392,16,64]{1,3,0,2:T(8,128)(2,1)} %bitcast.24), calls=%async_computation.1 | async-start | bytes 2097152 | tf_op jit(solution)/shard_map/all_to_all | solution.py:88
  105.3 29.8 %all-to-all-start.2 = ((bf16[1,392,16,64]{1,3,0,2:T(8,128)(2,1)}), bf16[1,392,16,64]{1,3,0,2:T(8,128)(2,1)}, u32[]{:S(2)}, u32[]{:S(2)}) async-start(bf16[1,392,16,64]{1,3,0,2:T(8,128)(2,1)} %bitcast.31), calls=%async_computation.2 | async-start | bytes 2097152 | tf_op jit(solution)/shard_map/all_to_all | solution.py:89
  109.6 132.6 %all-gather.17.cloned.1.call-start = ((), (), s32[]{:S(2)}) async-start(), calls=%async_computation.20 | async-start | bytes 9437184 | tf_op jit(solution)/shard_map/all_gather | solution.py:156
  174.5 36.3 %copy-start.14 = (f32[1024]{0:T(1024)S(1)}, f32[1024]{0:T(1024)}, u32[]{:S(2)}) copy-start(f32[1024]{0:T(1024)} %param.34) | copy-start | bytes 12292
  178.4 24.5 %all-to-all-start.4 = ((bf16[4,2,50176]{2,1,0:T(2,128)(2,1)}), bf16[4,2,50176]{2,1,0:T(2,128)(2,1)}, u32[]{:S(2)}, u32[]{:S(2)}) async-start(bf16[4,2,50176]{2,1,0:T(2,128)(2,1)} %reshape.300), calls=%async_computation.4 | async-start | bytes 1605632 | tf_op jit(solution)/shard_map/all_to_all | solution.py:95
  214.1 44.4 %copy-start.21 = (f32[392]{0:T(512)}, f32[392]{0:T(512)S(1)}, u32[]{:S(2)}) copy-start(f32[392]{0:T(512)S(1)} %broadcast_multiply_fusion.4) | copy-start | bytes 4708
  215.6 42.9 %copy-start.28 = (f32[392]{0:T(512)}, f32[392]{0:T(512)S(1)}, u32[]{:S(2)}) copy-start(f32[392]{0:T(512)S(1)} %add_rsqrt_fusion) | copy-start | bytes 4708
  265.1 44.0 %all-to-all-start.5 = ((bf16[1,392,16,64]{1,3,0,2:T(8,128)(2,1)}), bf16[1,392,16,64]{1,3,0,2:T(8,128)(2,1)}, u32[]{:S(2)}, u32[]{:S(2)}) async-start(bf16[1,392,16,64]{1,3,0,2:T(8,128)(2,1)} %bitcast.308), calls=%async_computation.5 | async-start | bytes 2097152 | tf_op jit(solution)/shard_map/all_to_all | solution.py:207
  269.7 544.2 %reduce-scatter.13.cloned.1.call-start = ((), (), s32[]{:S(2)}) async-start(), calls=%async_computation.24 | async-start | bytes 4325376 | tf_op jit(solution)/shard_map/reduce_scatter | solution.py:270
  274.7 539.2 %reduce-scatter.7.cloned.1.call-start = ((), (), s32[]{:S(2)}) async-start(), calls=%async_computation.21 | async-start | bytes 4325376 | tf_op jit(solution)/shard_map/reduce_scatter | solution.py:265
  453.1 33.3 %copy-start.31 = (f32[1024]{0:T(1024)S(1)}, f32[1024]{0:T(1024)}, u32[]{:S(2)}) copy-start(f32[1024]{0:T(1024)} %param.26) | copy-start | bytes 12292
  453.1 33.3 %copy-start.43 = (f32[1024]{0:T(1024)S(1)}, f32[1024]{0:T(1024)}, u32[]{:S(2)}) copy-start(f32[1024]{0:T(1024)} %param.27) | copy-start | bytes 12292
  491.5 322.4 %reduce-scatter.9.cloned.1.call-start = ((), (), s32[]{:S(2)}) async-start(), calls=%async_computation.22 | async-start | bytes 4325376 | tf_op jit(solution)/shard_map/reduce_scatter | solution.py:267
  555.5 396.6 %reduce-scatter.11.cloned.1.call-start = ((), (), s32[]{:S(2)}) async-start(), calls=%async_computation.23 | async-start | bytes 4325376 | tf_op jit(solution)/shard_map/reduce_scatter | solution.py:268
  618.3 699.6 %reduce-scatter.15.cloned.1.call-start = ((), (), s32[]{:S(2)}) async-start(), calls=%async_computation.25 | async-start | bytes 17301504 | tf_op jit(solution)/shard_map/reduce_scatter | solution.py:274
  632.0 1050.8 %reduce-scatter.17.cloned.1.call-start = ((), (), s32[]{:S(2)}) async-start(), calls=%async_computation.26 | async-start | bytes 17301504 | tf_op jit(solution)/shard_map/reduce_scatter | solution.py:276
  686.8 40.2 %copy-start.3 = (bf16[1,392,1024]{2,1,0:T(8,128)(2,1)S(1)}, bf16[1,392,1024]{2,1,0:T(8,128)(2,1)}, u32[]{:S(2)}) copy-start(bf16[1,392,1024]{2,1,0:T(8,128)(2,1)} %param.24) | copy-start | bytes 2408452
  686.8 40.2 %copy-start.15 = (f32[1024]{0:T(1024)S(1)}, f32[1024]{0:T(1024)}, u32[]{:S(2)}) copy-start(f32[1024]{0:T(1024)} %param.34) | copy-start | bytes 12292
  686.8 37.4 %all-to-all-start.3 = ((bf16[4,2,50176]{2,1,0:T(2,128)(2,1)}), bf16[4,2,50176]{2,1,0:T(2,128)(2,1)S(1)}, u32[]{:S(2)}, u32[]{:S(2)}) async-start(bf16[4,2,50176]{2,1,0:T(2,128)(2,1)} %reshape.298), calls=%async_computation.3 | async-start | bytes 1605632 | tf_op jit(solution)/shard_map/all_to_all | solution.py:95
  763.5 47.3 %copy-start.7 = (f32[392,1024]{1,0:T(8,128)S(1)}, f32[392,1024]{1,0:T(8,128)}, u32[]{:S(2)}) copy-start(f32[392,1024]{1,0:T(8,128)} %copy-done.6) | copy-start | bytes 4816900
  (41 other events, 260.3 us)
Sparse Core Ops, SparseCore 0:
  9.9 30.5 all-gather.6
  42.4 27.8 all-gather.8
  72.2 27.8 all-gather.10
  101.9 27.8 all-gather.12
  131.6 54.4 all-gather.14
  187.8 54.3 all-gather.16
  274.8 153.5 reduce-scatter.12
  491.7 155.6 reduce-scatter.6
  650.2 152.9 reduce-scatter.8
  805.8 146.1 reduce-scatter.10
  954.9 362.8 reduce-scatter.14
  1320.6 362.1 reduce-scatter.16
where the time goes:
time: 1700 us; the launch traced here: 1690 us
  waiting for transfers between devices  1060 us (62%)
  matrix products  265 us (16%)
  blocking collectives  140 us (8%)
  local copies, waits for them, and re-layouts  119 us (7%)
  other arithmetic  65.8 us (4%)
  starting transfers between devices  26.8 us (2%)
    reduce_scatter x1, waiting for transfers between devices, on_device(): lax.psum_scatter(all_grads[11], ('fsdp', 'seq'), scatter_dimension=0, til...  366 us
    reduce_scatter x1, waiting for transfers between devices, on_device(): lax.psum_scatter(all_grads[13], ('fsdp', 'seq'), scatter_dimension=0, til...  365 us
    reduce_scatter x1, waiting for transfers between devices, on_device(): lax.psum_scatter(all_grads[5], ('fsdp', 'seq'), scatter_dimension=0, tile...  138 us
    unnamed x118, local copies, waits for them, and re-layouts  58 us
    all_to_all x2, waiting for transfers between devices, run_forward(): lax.all_to_all(from_pairs(mixed_pairs, clips), 'seq', split_axis=1, conca...  52.8 us
    convert_element_type x4, other arithmetic, head_backward(): grad_scores = (probs * (grad_probs - inner)).astype(jnp.bfloat16)  41.9 us
    all_to_all x1, blocking collectives, on_device(): lax.all_to_all(from_pairs(grad_k_pairs, clips), 'seq', split_axis=1, conc...  40.5 us
    all_to_all x1, blocking collectives, on_device(): lax.all_to_all(from_pairs(grad_v_pairs, clips), 'seq', split_axis=1, conc...  39.4 us
  transfers between devices with their start and end apart: 18, of which 13 were waited for; matrix products, arithmetic and copies ran while one was open for 25% of the time, Pallas kernels for 0%

commit v1 on v0

--- a/solution.py
+++ b/solution.py
@@ -92,8 +92,14 @@
     keys_pairs = to_pairs(keys_heads)
     values_pairs = to_pairs(values_heads)
     mixed_pairs, logsum = lax.map(head_forward, (query_pairs, keys_pairs, values_pairs))
-    mixed_tokens = lax.all_to_all(
-        from_pairs(mixed_pairs, clips), "seq", split_axis=1, concat_axis=2, tiled=True
+    mixed_tokens = jnp.concatenate(
+        lax.all_to_all(
+            jnp.stack(jnp.split(from_pairs(mixed_pairs, clips), lax.axis_size("seq"), axis=1)),
+            "seq",
+            0,
+            0,
+        ),
+        axis=2,
     )
     attended = mixed_tokens.reshape(clips * local_len, width)
     branch = jnp.dot(attended, w_out, preferred_element_type=jnp.float32) + b_out

time: 1700 us -> 1710 us (level)
  waiting for transfers between devices: 1060 us -> 1090 us
  local copies, waits for them, and re-layouts: 119 us -> 90.9 us
    unnamed x118 -> x112, local copies, waits for them, and re-layouts: 58 us -> 39.6 us
  transfers between devices with their start and end apart: 18 -> 18, of which waited for: 13 -> 13; matrix products, arithmetic and copies ran while one was open for 25% -> 23% of each run, Pallas kernels for 0% -> 0%
where the time goes in v1:
time: 1710 us; the launch traced here: 1700 us
  waiting for transfers between devices  1090 us (64%)
  matrix products  265 us (15%)
  blocking collectives  142 us (8%)
  local copies, waits for them, and re-layouts  90.9 us (5%)
  other arithmetic  68.1 us (4%)
  starting transfers between devices  27 us (2%)
    reduce_scatter x1, waiting for transfers between devices, on_device(): lax.psum_scatter(all_grads[11], ('fsdp', 'seq'), scatter_dimension=0, til...  365 us
    reduce_scatter x1, waiting for transfers between devices, on_device(): lax.psum_scatter(all_grads[13], ('fsdp', 'seq'), scatter_dimension=0, til...  365 us
    reduce_scatter x1, waiting for transfers between devices, on_device(): lax.psum_scatter(all_grads[5], ('fsdp', 'seq'), scatter_dimension=0, tile...  146 us
    all_to_all x2, waiting for transfers between devices, run_forward(): lax.all_to_all(jnp.stack(jnp.split(from_pairs(mixed_pairs, clips), lax.ax...  64.4 us
    convert_element_type x4, other arithmetic, head_backward(): grad_scores = (probs * (grad_probs - inner)).astype(jnp.bfloat16)  42 us
    unnamed x1, blocking collectives  41 us
    all_to_all x1, blocking collectives, on_device(): lax.all_to_all(from_pairs(grad_k_pairs, clips), 'seq', split_axis=1, conc...  40.4 us
    unnamed x112, local copies, waits for them, and re-layouts  39.6 us
  transfers between devices with their start and end apart: 18, of which 13 were waited for; matrix products, arithmetic and copies ran while one was open for 23% of the time, Pallas kernels for 0%

profile of v1, /device:TPU:0, one launch (start us, length us, event | category | flops | bytes accessed | tf_op | source)
XLA Modules:
  0.0 1695.7 jit_solution(17899123755745325068)
XLA Ops:
  13.5 27.1 %all-gather.7.cloned.1.call-done = bf16[1024,1024]{1,0:T(8,128)(2,1)} async-done(((bf16[128,1024]{1,0:T(8,128)(2,1)}), bf16[1024,1024]{1,0:T(8,128)(2,1)}) %all-gather.7.cloned.1.call-update) | async-done | bytes 2097168 | tf_op jit(solution)/shard_map/all_gather | solution.py:155
  49.5 20.9 %all-gather.9.cloned.1.call-done = bf16[1024,1024]{1,0:T(8,128)(2,1)} async-done(((bf16[128,1024]{1,0:T(8,128)(2,1)}), bf16[1024,1024]{1,0:T(8,128)(2,1)}) %all-gather.9.cloned.1.call-update) | async-done | bytes 2097168 | tf_op jit(solution)/shard_map/all_gather | solution.py:156
  79.8 20.3 %all-gather.11.cloned.1.call-done = bf16[1024,1024]{1,0:T(8,128)(2,1)} async-done(((bf16[128,1024]{1,0:T(8,128)(2,1)}), bf16[1024,1024]{1,0:T(8,128)(2,1)}) %all-gather.11.cloned.1.call-update) | async-done | bytes 2097168 | tf_op jit(solution)/shard_map/all_gather | solution.py:157
  113.1 22.1 %all-to-all-done.2 = bf16[1,392,16,64]{1,3,0,2:T(8,128)(2,1)} async-done(((bf16[1,392,16,64]{1,3,0,2:T(8,128)(2,1)}), bf16[1,392,16,64]{1,3,0,2:T(8,128)(2,1)}, u32[]{:S(2)}, u32[]{:S(2)}) %all-to-all-start.2) | async-done | bytes 802848 | tf_op jit(solution)/shard_map/all_to_all | solution.py:89
  138.7 29.4 %while.37 = (s32[]{:T(128)}, bf16[4,1568,64]{1,2,0:T(8,128)(2,1)}, f32[4,1568]{1,0:T(4,128)S(1)}, bf16[4,1568,64]{2,1,0:T(8,128)(2,1)S(1)}, bf16[4,1568,64]{2,1,...) while((s32[]{:T(128)}, bf16[4,1568,64]{1,2,0:T(8,128)(2,1)}, ...), condition=%wide.region_11.12_spmd, body=%wide.region_8.0_spmd.sunk | while | flops 651634176 | bytes 30998112 | solution.py:94
  176.2 24.8 %all-to-all-done.4 = bf16[4,1,392,4,64]{2,4,3,1,0:T(8,128)(2,1)} async-done(((bf16[4,1,392,4,64]{2,4,3,1,0:T(8,128)(2,1)}), bf16[4,1,392,4,64]{2,4,3,1,0:T(8,128)(2,1)}, u32[]{:S(2)}, u32[]{:S(2)}) %all-to-all-start.4) | async-done | bytes 802848 | tf_op jit(solution)/shard_map/all_to_all | solution.py:96
  205.8 21.0 %fusion.70 = (f32[392,4096]{1,0:T(8,128)}, f32[392,4096]{1,0:T(8,128)}) fusion(f32[4096]{0:T(1024)S(1)} %copy-done.16, bf16[1024,4096]{1,0:T(8,128)(2,1)} %all-gather.15.cloned.1.call-done, f32[392,1024]{1,0:T(8,128)} %copy-done.4, f32[392]{0:T(512)S(1)} %add_rsqrt_fusion, f32[392]{0:T(512)S(1)} %broadcast_multiply_fusion.4, f32[1024]{0:T(1024)S(1)} %copy-done.45, ...), kind=kOutput, calls=%fused_computation.79 | convolution fusion | flops 3391496192 | bytes 22867008 | tf_op jit(solution)/shard_map/dot_general | solution.py:109
  226.7 15.4 all-gather.17.cloned.1.call-done
  242.2 11.6 convert_reduce_fusion
  274.5 34.4 %all-to-all-done.5 = bf16[1,392,16,64]{1,3,0,2:T(8,128)(2,1)} async-done(((bf16[1,392,16,64]{1,3,0,2:T(8,128)(2,1)}), bf16[1,392,16,64]{1,3,0,2:T(8,128)(2,1)}, u32[]{:S(2)}, u32[]{:S(2)}) %all-to-all-start.5) | async-done | bytes 802848 | tf_op jit(solution)/shard_map/all_to_all | solution.py:213
  314.6 132.6 %while.38 = (s32[]{:T(128)}, bf16[4,1568,64]{1,2,0:T(8,128)(2,1)}, bf16[4,1568,64]{1,2,0:T(8,128)(2,1)}, bf16[4,1568,64]{1,2,0:T(8,128)(2,1)}, bf16[4,1568,64]{2...) while((s32[]{:T(128)}, bf16[4,1568,64]{1,2,0:T(8,128)(2,1)}, ...), condition=%wide.region_18.19_spmd, body=%wide.region_16.18_spmd.sunk | while | flops 1593688576 | bytes 138059424 | solution.py:220
  324.3 10.5 multiply_convert_fusion.5
  341.4 6.4 fusion.259
  357.4 10.5 multiply_convert_fusion.5
  374.6 6.3 fusion.259
  383.6 5.8 multiply_reduce_fusion.14
  390.6 10.5 multiply_convert_fusion.5
  407.8 6.3 fusion.259
  423.8 10.5 multiply_convert_fusion.5
  440.9 6.3 fusion.259
  457.5 21.2 %all_to_all.142 = bf16[4,2,50176]{2,1,0:T(2,128)(2,1)} all-to-all(bf16[4,2,50176]{2,1,0:T(2,128)(2,1)} %reshape.296), channel_id=1, replica_groups=mesh['fsdp'=8,'seq'=4] {'seq'}, dimensions={0} | all-to-all | bytes 1605632 | tf_op jit(solution)/shard_map/all_to_all | solution.py:224
  502.2 40.4 %all_to_all.143 = bf16[4,2,50176]{2,1,0:T(2,128)(2,1)} all-to-all(bf16[4,2,50176]{2,1,0:T(2,128)(2,1)} %reshape.298), channel_id=1, replica_groups=mesh['fsdp'=8,'seq'=4] {'seq'}, dimensions={0} | all-to-all | bytes 1605632 | tf_op jit(solution)/shard_map/all_to_all | solution.py:227
  566.0 39.2 %all_to_all.144 = bf16[4,2,50176]{2,1,0:T(2,128)(2,1)} all-to-all(bf16[4,2,50176]{2,1,0:T(2,128)(2,1)} %reshape.300), channel_id=1, replica_groups=mesh['fsdp'=8,'seq'=4] {'seq'}, dimensions={0} | all-to-all | bytes 1605632 | tf_op jit(solution)/shard_map/all_to_all | solution.py:230
  618.4 13.0 fusion.182
  632.1 15.5 fusion.83
  648.6 28.9 %while.36 = (s32[]{:T(128)}, bf16[4,1568,64]{1,2,0:T(8,128)(2,1)}, bf16[4,1568,64]{2,1,0:T(8,128)(2,1)S(1)}, bf16[4,1568,64]{2,1,0:T(8,128)(2,1)S(1)}, bf16[4,1568,64]{2,1,0:T(8,128)(2,1)}, /*index=5*/s32[]{:T(128)}) while((s32[]{:T(128)}, bf16[4,1568,64]{1,2,0:T(8,128)(2,1)}, bf16[4,1568,64]{2,1,0:T(8,128)(2,1)S(1)}, ...), condition=%wide.region_5.6_spmd, body=%wide.region_2.5_spmd.sunk | while | flops 651632576 | bytes 30954188 | solution.py:94
  684.4 39.6 %all-to-all-done.3 = bf16[4,1,392,4,64]{2,4,3,1,0:T(8,128)(2,1)S(1)} async-done(((bf16[4,1,392,4,64]{2,4,3,1,0:T(8,128)(2,1)}), bf16[4,1,392,4,64]{2,4,3,1,0:T(8,128)(2,1)S(1)}, u32[]{:S(2)}, u32[]{:S(2)}) %all-to-all-start.3) | async-done | bytes 802848 | tf_op jit(solution)/shard_map/all_to_all | solution.py:96
  727.1 26.4 %fusion.137 = bf16[1,392,1024]{2,1,0:T(8,128)(2,1)} fusion(f32[392,1024]{1,0:T(8,128)S(1)} %get-tuple-element.206, bf16[4096,1024]{1,0:T(8,128)(2,1)} %all-gather.17.cloned.1.call-done, bf16[1024,4096]{1,0:T(8,128)(2,1)} %all-gather.15.cloned.1.call-done, f32[4096]{0:T(1024)S(1)} %copy-done.17, f32[]{:T(128)} %bitcast.46, f32[1024]{0:T(1024)S(1)} %copy-done.44, ...), kind=kOutput, calls=%fused_computation.189 | convolution fusion | flops 6686253056 | bytes 19217476 | tf_op jit(solution)/shard_map/dot_general | solution.py:111
  763.0 41.0 %all-reduce.9 = (f32[1024]{0:T(1024)S(1)}, f32[1024]{0:T(1024)S(1)}, f32[1024]{0:T(1024)S(1)}, f32[1024]{0:T(1024)S(1)}, f32[1024]{0:T(1024)S(1)}, /*index=5*/f3...) all-reduce(f32[1024]{0:T(1024)S(1)} %get-tuple-element.134, ...), channel_id=2, replica_groups=mesh['fsdp'=8,'seq'=4] {'fsdp','seq'}, use_global_device_ids=true, to_apply=%region_22.23.clone | all-reduce | flops 12288 | bytes 98304
  812.4 145.7 %reduce-scatter.11.cloned.1.call-done = f32[32,1024]{1,0:T(8,128)} async-done(((f32[1024,1024]{1,0:T(8,128)}), f32[32,1024]{1,0:T(8,128)}) %reduce-scatter.11.cloned.1.call-update) | async-done | bytes 131088 | tf_op jit(solution)/shard_map/reduce_scatter | solution.py:274
  958.1 365.4 %reduce-scatter.15.cloned.1.call-done = f32[32,4096]{1,0:T(8,128)} async-done(((f32[1024,4096]{1,0:T(8,128)}), f32[32,4096]{1,0:T(8,128)}) %reduce-scatter.15.cloned.1.call-update) | async-done | bytes 524304 | tf_op jit(solution)/shard_map/reduce_scatter | solution.py:280
  1323.6 364.9 %reduce-scatter.17.cloned.1.call-done = f32[128,1024]{1,0:T(8,128)} async-done(((f32[4096,1024]{1,0:T(8,128)}), f32[128,1024]{1,0:T(8,128)}) %reduce-scatter.17.cloned.1.call-update) | async-done | bytes 524304 | tf_op jit(solution)/shard_map/reduce_scatter | solution.py:282
  (278 shorter events, 296.7 us)
Async XLA Ops:
  7.2 33.4 %all-gather.7.cloned.1.call-start = ((), (), s32[]{:S(2)}) async-start(), calls=%async_computation.15 | async-start | bytes 2359296 | tf_op jit(solution)/shard_map/all_gather | solution.py:155
  7.9 62.4 %all-gather.9.cloned.1.call-start = ((), (), s32[]{:S(2)}) async-start(), calls=%async_computation.16 | async-start | bytes 2359296 | tf_op jit(solution)/shard_map/all_gather | solution.py:156
  8.7 91.5 %all-gather.11.cloned.1.call-start = ((), (), s32[]{:S(2)}) async-start(), calls=%async_computation.17 | async-start | bytes 2359296 | tf_op jit(solution)/shard_map/all_gather | solution.py:157
  9.4 166.8 %all-gather.13.cloned.1.call-start = ((), (), s32[]{:S(2)}) async-start(), calls=%async_computation.18 | async-start | bytes 2359296 | tf_op jit(solution)/shard_map/all_gather | solution.py:158
  10.0 195.8 %all-gather.15.cloned.1.call-start = ((), (), s32[]{:S(2)}) async-start(), calls=%async_computation.19 | async-start | bytes 9437184 | tf_op jit(solution)/shard_map/all_gather | solution.py:161
  11.9 88.3 %copy-start.18 = (f32[392]{0:T(512)}, f32[392]{0:T(512)S(1)}, u32[]{:S(2)}) copy-start(f32[392]{0:T(512)S(1)} %broadcast_multiply_fusion.6) | copy-start | bytes 4708
  13.4 86.8 %copy-start.25 = (f32[392]{0:T(512)}, f32[392]{0:T(512)S(1)}, u32[]{:S(2)}) copy-start(f32[392]{0:T(512)S(1)} %add_rsqrt_fusion.2) | copy-start | bytes 4708
  13.4 56.9 %copy-start.2 = (bf16[1,392,1024]{2,1,0:T(8,128)(2,1)S(1)}, bf16[1,392,1024]{2,1,0:T(8,128)(2,1)}, u32[]{:S(2)}) copy-start(bf16[1,392,1024]{2,1,0:T(8,128)(2,1)} %param.24) | copy-start | bytes 2408452
  13.4 56.9 %copy-start.30 = (f32[1024]{0:T(1024)S(1)}, f32[1024]{0:T(1024)}, u32[]{:S(2)}) copy-start(f32[1024]{0:T(1024)} %param.26) | copy-start | bytes 12292
  13.4 56.9 %copy-start.42 = (f32[1024]{0:T(1024)S(1)}, f32[1024]{0:T(1024)}, u32[]{:S(2)}) copy-start(f32[1024]{0:T(1024)} %param.27) | copy-start | bytes 12292
  44.9 30.8 %all-to-all-start = ((bf16[1,392,16,64]{1,3,0,2:T(8,128)(2,1)}), bf16[1,392,16,64]{1,3,0,2:T(8,128)(2,1)S(1)}, u32[]{:S(2)}, u32[]{:S(2)}) async-start(bf16[1,392,16,64]{1,3,0,2:T(8,128)(2,1)} %bitcast.17), calls=%async_computation | async-start | bytes 2097152 | tf_op jit(solution)/shard_map/all_to_all | solution.py:87
  49.4 50.7 %copy-start.41 = (f32[1024]{0:T(1024)S(1)}, f32[1024]{0:T(1024)}, u32[]{:S(2)}) copy-start(f32[1024]{0:T(1024)} %param.32) | copy-start | bytes 12292
  75.6 29.7 %all-to-all-start.1 = ((bf16[1,392,16,64]{1,3,0,2:T(8,128)(2,1)}), bf16[1,392,16,64]{1,3,0,2:T(8,128)(2,1)}, u32[]{:S(2)}, u32[]{:S(2)}) async-start(bf16[1,392,16,64]{1,3,0,2:T(8,128)(2,1)} %bitcast.24), calls=%async_computation.1 | async-start | bytes 2097152 | tf_op jit(solution)/shard_map/all_to_all | solution.py:88
  105.3 29.8 %all-to-all-start.2 = ((bf16[1,392,16,64]{1,3,0,2:T(8,128)(2,1)}), bf16[1,392,16,64]{1,3,0,2:T(8,128)(2,1)}, u32[]{:S(2)}, u32[]{:S(2)}) async-start(bf16[1,392,16,64]{1,3,0,2:T(8,128)(2,1)} %bitcast.31), calls=%async_computation.2 | async-start | bytes 2097152 | tf_op jit(solution)/shard_map/all_to_all | solution.py:89
  109.6 132.6 %all-gather.17.cloned.1.call-start = ((), (), s32[]{:S(2)}) async-start(), calls=%async_computation.20 | async-start | bytes 9437184 | tf_op jit(solution)/shard_map/all_gather | solution.py:162
  170.9 30.1 %all-to-all-start.4 = ((bf16[4,1,392,4,64]{2,4,3,1,0:T(8,128)(2,1)}), bf16[4,1,392,4,64]{2,4,3,1,0:T(8,128)(2,1)}, u32[]{:S(2)}, u32[]{:S(2)}) async-start(bf16[4,1,392,4,64]{2,4,3,1,0:T(8,128)(2,1)} %pad_maximum_fusion.1), calls=%async_computation.4 | async-start | bytes 2097152 | tf_op jit(solution)/shard_map/all_to_all | solution.py:96
  204.2 54.0 %copy-start.21 = (f32[392]{0:T(512)}, f32[392]{0:T(512)S(1)}, u32[]{:S(2)}) copy-start(f32[392]{0:T(512)S(1)} %broadcast_multiply_fusion.4) | copy-start | bytes 4708
  205.7 52.5 %copy-start.28 = (f32[392]{0:T(512)}, f32[392]{0:T(512)S(1)}, u32[]{:S(2)}) copy-start(f32[392]{0:T(512)S(1)} %add_rsqrt_fusion) | copy-start | bytes 4708
  264.8 44.0 %all-to-all-start.5 = ((bf16[1,392,16,64]{1,3,0,2:T(8,128)(2,1)}), bf16[1,392,16,64]{1,3,0,2:T(8,128)(2,1)}, u32[]{:S(2)}, u32[]{:S(2)}) async-start(bf16[1,392,16,64]{1,3,0,2:T(8,128)(2,1)} %bitcast.312), calls=%async_computation.5 | async-start | bytes 2097152 | tf_op jit(solution)/shard_map/all_to_all | solution.py:213
  269.5 542.9 %reduce-scatter.13.cloned.1.call-start = ((), (), s32[]{:S(2)}) async-start(), calls=%async_computation.24 | async-start | bytes 4325376 | tf_op jit(solution)/shard_map/reduce_scatter | solution.py:276
  274.5 537.9 %reduce-scatter.7.cloned.1.call-start = ((), (), s32[]{:S(2)}) async-start(), calls=%async_computation.21 | async-start | bytes 4325376 | tf_op jit(solution)/shard_map/reduce_scatter | solution.py:271
  491.8 320.5 %reduce-scatter.9.cloned.1.call-start = ((), (), s32[]{:S(2)}) async-start(), calls=%async_computation.22 | async-start | bytes 4325376 | tf_op jit(solution)/shard_map/reduce_scatter | solution.py:273
  555.7 402.5 %reduce-scatter.11.cloned.1.call-start = ((), (), s32[]{:S(2)}) async-start(), calls=%async_computation.23 | async-start | bytes 4325376 | tf_op jit(solution)/shard_map/reduce_scatter | solution.py:274
  618.3 705.2 %reduce-scatter.15.cloned.1.call-start = ((), (), s32[]{:S(2)}) async-start(), calls=%async_computation.25 | async-start | bytes 17301504 | tf_op jit(solution)/shard_map/reduce_scatter | solution.py:280
  631.4 1057.1 %reduce-scatter.17.cloned.1.call-start = ((), (), s32[]{:S(2)}) async-start(), calls=%async_computation.26 | async-start | bytes 17301504 | tf_op jit(solution)/shard_map/reduce_scatter | solution.py:282
  677.5 46.5 %copy-start.3 = (bf16[1,392,1024]{2,1,0:T(8,128)(2,1)S(1)}, bf16[1,392,1024]{2,1,0:T(8,128)(2,1)}, u32[]{:S(2)}) copy-start(bf16[1,392,1024]{2,1,0:T(8,128)(2,1)} %param.24) | copy-start | bytes 2408452
  677.5 46.5 %copy-start.15 = (f32[1024]{0:T(1024)S(1)}, f32[1024]{0:T(1024)}, u32[]{:S(2)}) copy-start(f32[1024]{0:T(1024)} %param.34) | copy-start | bytes 12292
  680.3 46.7 %copy-start.37 = (f32[1024]{0:T(1024)S(1)}, f32[1024]{0:T(1024)}, u32[]{:S(2)}) copy-start(f32[1024]{0:T(1024)} %param.35) | copy-start | bytes 12292
  680.3 46.7 %copy-start.44 = (f32[1024]{0:T(1024)S(1)}, f32[1024]{0:T(1024)}, u32[]{:S(2)}) copy-start(f32[1024]{0:T(1024)} %param.40) | copy-start | bytes 12292
  680.3 46.7 %copy-start.47 = (f32[1024]{0:T(1024)S(1)}, f32[1024]{0:T(1024)}, u32[]{:S(2)}) copy-start(f32[1024]{0:T(1024)} %param.36) | copy-start | bytes 12292
  680.3 43.6 %all-to-all-start.3 = ((bf16[4,1,392,4,64]{2,4,3,1,0:T(8,128)(2,1)}), bf16[4,1,392,4,64]{2,4,3,1,0:T(8,128)(2,1)S(1)}, u32[]{:S(2)}, u32[]{:S(2)}) async-start(bf16[4,1,392,4,64]{2,4,3,1,0:T(8,128)(2,1)} %pad_maximum_fusion), calls=%async_computation.3 | async-start | bytes 2097152 | tf_op jit(solution)/shard_map/all_to_all | solution.py:96
  760.0 49.3 %copy-start.7 = (f32[392,1024]{1,0:T(8,128)S(1)}, f32[392,1024]{1,0:T(8,128)}, u32[]{:S(2)}) copy-start(f32[392,1024]{1,0:T(8,128)} %copy-done.6) | copy-start | bytes 4816900
  (41 other events, 450.2 us)
Sparse Core Ops, SparseCore 0:
  9.9 30.5 all-gather.6
  42.4 27.8 all-gather.8
  72.2 27.8 all-gather.10
  101.9 27.8 all-gather.12
  131.6 54.4 all-gather.14
  187.8 54.3 all-gather.16
  274.6 153.7 reduce-scatter.12
  492.0 155.7 reduce-scatter.6
  650.6 157.4 reduce-scatter.8
  810.8 147.2 reduce-scatter.10
  961.0 362.5 reduce-scatter.14
  1326.3 362.1 reduce-scatter.16
